TPU v7x, 256 devices: a whole 4x4x8 slice. The times are simulated.
256 devices in a mesh: dp: 2 (over core), seq: 8 (over z), expert: 16 (over y, x).
Axes of the slice: x: 4, y: 4, z: 8, core: 2. Of those that a mesh axis runs over, the one named last changes fastest.
Arguments:
- tokens: bfloat16 [16384, 2048], P(('dp', 'seq')), may hold values from -6 to 6
- phi: bfloat16 [2048, 32], P(None, 'expert'), may hold values from -40 to 40
- w_in: bfloat16 [32, 2048, 8192], P('expert', None, ('dp', 'seq')), may hold values from -1 to 1
- w_out: bfloat16 [32, 8192, 2048], P('expert', ('dp', 'seq')), may hold values from -0.25 to 0.25
Outputs:
- mixed: bfloat16 [16384, 2048], P(('dp', 'seq', 'expert'))
All inputs are finite; a program needn't handle non-finite values.
Results may differ from a plain program's by a relative error of at most 0.0068.
Values may be sent and summed in bfloat16 or wider, within the bound.
A program may use at most 64 MiB of HBM per device.

v0:
```python
import jax
import jax.numpy as jnp
from jax import lax
from jax.sharding import PartitionSpec as P


def on_device(tokens, phi, w_in, w_out):
    logits = lax.dot_general(
        phi, tokens, (((0,), (1,)), ((), ())), preferred_element_type=jnp.float32
    )
    slot_max = lax.pmax(jnp.max(logits, axis=1), "seq")
    spread = jnp.exp(logits - slot_max[:, None])
    numerator = jnp.dot(spread.astype(jnp.bfloat16), tokens, preferred_element_type=jnp.float32)
    denominator = jnp.sum(spread, axis=1)
    numer_seq, denom_seq = lax.psum((numerator, denominator), "seq")
    own_slots = (numer_seq / denom_seq[:, None]).astype(jnp.bfloat16)
    slot_in = lax.all_gather(own_slots[None], "dp", axis=0, tiled=True)
    hidden = jax.nn.gelu(
        jnp.einsum("ced,edf->cef", slot_in, w_in, preferred_element_type=jnp.float32),
        approximate=True,
    ).astype(jnp.bfloat16)
    partial_value = jnp.einsum("cef,efd->ced", hidden, w_out, preferred_element_type=jnp.float32)
    totals = lax.psum(partial_value, ("dp", "seq"))
    summed = lax.dynamic_index_in_dim(totals, lax.axis_index("dp"), 0, keepdims=False)
    slot_out = summed.astype(jnp.bfloat16)
    row_max = lax.pmax(jnp.max(logits, axis=0), "expert")
    combine_weights = jnp.exp(logits - row_max[None, :])
    local_numer = lax.dot_general(
        combine_weights.astype(jnp.bfloat16),
        slot_out,
        (((0,), (0,)), ((), ())),
        preferred_element_type=jnp.float32,
    )
    mixed_numer, mixed_denom = (
        lax.psum_scatter(local_numer, "expert", scatter_dimension=0, tiled=True),
        lax.psum_scatter(
            jnp.sum(combine_weights, axis=0), "expert", scatter_dimension=0, tiled=True
        ),
    )
    return (mixed_numer / mixed_denom[:, None]).astype(jnp.bfloat16)


def solution(mesh):
    placed = (
        P(("dp", "seq"), None),
        P(None, "expert"),
        P("expert", None, ("dp", "seq")),
        P("expert", ("dp", "seq"), None),
    )
    return jax.shard_map(
        on_device,
        mesh=mesh,
        in_specs=placed,
        out_specs=P(("dp", "seq", "expert"), None),
        check_vma=False,
    )
```

profile of v0, /device:TPU:2, one launch (start us, length us, event | category | flops | bytes accessed | tf_op | source)
XLA Modules:
  0.0 258.3 jit_solution(14364468299653725748)
XLA Ops:
  6.5 0.0 copy-start
  6.5 0.0 reduce-scatter.2.cloned.1.call-start
  6.5 0.7 copy-done
  7.2 3.5 %fusion.35 = (f32[1024]{0:T(1024)S(1)}, f32[2]{0:T(128)S(1)}, f32[2,1024]{1,0:T(2,128)S(1)}) fusion(bf16[2048,2]{0,1:T(2,128)(2,1)S(1)} %copy-done, bf16[1024,2048]{1,0:T(8,128)(2,1)} %param.4), kind=kOutput, calls=%fused_computation.35 | convolution fusion | flops 8391678 | bytes 4214792 | tf_op jit(solution)/shard_map/dot_general | solution.py:8
  10.7 37.7 %pmax.14 = f32[1024]{0:T(1024)S(1)} all-reduce(f32[1024]{0:T(1024)S(1)} %get-tuple-element.7), channel_id=1, replica_groups=mesh['dp'=2,'seq'=8,'expert'=16] {'expert'}, use_global_device_ids=true, to_apply=%region_1.0 | all-reduce | flops 1024 | bytes 8192 | tf_op jit(solution)/shard_map/pmax | solution.py:26
  48.4 19.0 %pmax.15 = f32[2]{0:T(128)S(1)} all-reduce(f32[2]{0:T(128)S(1)} %get-tuple-element.8), channel_id=1, replica_groups=mesh['dp'=2,'seq'=8,'expert'=16] {'seq'}, use_global_device_ids=true, to_apply=%region_3.0 | all-reduce | flops 2 | bytes 16 | tf_op jit(solution)/shard_map/pmax | solution.py:11
  67.4 2.9 %fusion.23 = f32[2,2048]{1,0:T(2,128)S(1)} fusion(bf16[1024,2048]{1,0:T(8,128)(2,1)} %param.4, f32[2,1024]{1,0:T(2,128)S(1)} %get-tuple-element.11, f32[2]{0:T(128)S(1)} %pmax.15), kind=kOutput, calls=%fused_computation.25 | convolution fusion | flops 8392704 | bytes 4218888 | tf_op jit(solution)/shard_map/dot_general | solution.py:13
  70.3 0.2 fusion.19
  70.5 27.1 %all-reduce.1 = (f32[2,2048]{1,0:T(2,128)S(1)}, f32[2]{0:T(128)S(1)}) all-reduce(f32[2,2048]{1,0:T(2,128)S(1)} %fusion.23, f32[2]{0:T(128)S(1)} %get-tuple-element.6), channel_id=1, replica_groups=mesh['dp'=2,'seq'=8,'expert'=16] {'seq'}, use_global_device_ids=true, to_apply=%region_4.0 | all-reduce | flops 4098 | bytes 32784 | tf_op jit(solution)/shard_map/psum | solution.py:15
  97.6 0.1 fusion.18
  97.6 1.8 all-gather.1
  99.4 4.7 %convolution_bitcast_fusion = f32[2,2,2048]{2,0,1:T(2,128)S(1)} fusion(bf16[2,512,2048]{2,1,0:T(8,128)(2,1)} %param.7, bf16[2,2048,512]{2,1,0:T(8,128)(2,1)} %param.6, bf16[2,2,2048]{2,1,0:T(2,128)(2,1)S(1)} %all-gather.1), kind=kOutput, calls=%fused_computation | convolution fusion | flops 16795648 | bytes 8437760 | tf_op jit(solution)/shard_map/cef,efd->ced/dot_general | solution.py:22
  104.1 50.2 %psum.23 = bf16[2,2,2048]{2,0,1:T(2,128)(2,1)S(1)} all-reduce(f32[2,2,2048]{2,0,1:T(2,128)S(1)} %convolution_bitcast_fusion), channel_id=1, replica_groups=mesh['dp'=2,'seq'=8,'expert'=16] {'dp','seq'}, use_global_device_ids=true, to_apply=%region_7.8 | all-reduce | flops 8192 | bytes 49152 | tf_op jit(solution)/shard_map/psum | solution.py:23
  154.3 4.5 %fusion.15 = f32[1024,2048]{1,0:T(8,128)} fusion(bf16[1,2,2048]{2,0,1:T(2,128)(2,1)S(1)} %dynamic-slice_convert_fusion, f32[2,1024]{1,0:T(2,128)S(1)} %get-tuple-element.11, f32[1024]{0:T(1024)S(1)} %pmax.14), kind=kOutput, calls=%fused_computation.15 | convolution fusion | flops 8392704 | bytes 8409088 | tf_op jit(solution)/shard_map/dot_general | solution.py:28
  158.9 0.0 copy-start.1
  158.9 0.0 reduce-scatter.2.cloned.1.call-update
  158.9 0.6 copy-done.1
  159.5 0.6 dynamic-slice
  160.8 40.2 %all-reduce = f32[1024]{0:T(1024)S(1)} all-reduce(f32[1024]{0:T(1024)S(1)} %get-tuple-element.5), channel_id=4, replica_groups=mesh['dp'=2,'seq'=8,'expert'=16] {'expert'}, use_global_device_ids=true, to_apply=%region_10.11.clone | all-reduce | flops 1024 | bytes 8192
  201.0 0.1 dynamic-slice.1
  201.1 48.5 %reduce-scatter.2.cloned.1.call-done = f32[64,2048]{1,0:T(8,128)} async-done(((f32[1024,2048]{1,0:T(8,128)}), f32[64,2048]{1,0:T(8,128)}) %reduce-scatter.2.cloned.1.call-update) | async-done | bytes 524304 | tf_op jit(solution)/shard_map/reduce_scatter | solution.py:35
  249.6 1.8 divide_convert_fusion
  (1 shorter events, 0.0 us)
Async XLA Ops:
  6.5 0.7 copy-start
  6.5 243.0 %reduce-scatter.2.cloned.1.call-start = ((), (), s32[]{:S(2)}) async-start(), calls=%async_computation.1 | async-start | bytes 8912896 | tf_op jit(solution)/shard_map/reduce_scatter | solution.py:35
  158.9 0.7 copy-start.1
Sparse Core Ops, SparseCore 0:
  159.0 90.5 reduce-scatter.1
where the time goes:
time: 259 us; the launch traced here: 258 us
  blocking collectives  176 us (68%)
  waiting for transfers between devices  48.5 us (19%)
  matrix products  15.6 us (6%)
  between operations  14.1 us (5%)
    psum x1, blocking collectives, on_device(): totals = lax.psum(partial_value, ('dp', 'seq'))  50.2 us
    reduce_scatter x1, waiting for transfers between devices, on_device(): lax.psum_scatter(local_numer, 'expert', scatter_dimension=0, tiled=True)  48.5 us
    unnamed x1, blocking collectives  40.2 us
    pmax x1, blocking collectives, on_device(): row_max = lax.pmax(jnp.max(logits, axis=0), 'expert')  37.7 us
    psum x1, blocking collectives, on_device(): numer_seq, denom_seq = lax.psum((numerator, denominator), 'seq')  27.1 us
    pmax x1, blocking collectives, on_device(): slot_max = lax.pmax(jnp.max(logits, axis=1), 'seq')  19 us
  transfers between devices with their start and end apart: 1, of which 1 were waited for; matrix products, arithmetic and copies ran while one was open for 0% of the time, Pallas kernels for 0%

commit v1 on v0

--- a/solution.py
+++ b/solution.py
@@ -20,7 +20,9 @@
         approximate=True,
     ).astype(jnp.bfloat16)
     partial_value = jnp.einsum("cef,efd->ced", hidden, w_out, preferred_element_type=jnp.float32)
-    totals = lax.psum(partial_value, ("dp", "seq"))
+    totals = partial_value
+    for mesh_axis in ("dp", "seq"):
+        totals = lax.psum(totals, mesh_axis)
     summed = lax.dynamic_index_in_dim(totals, lax.axis_index("dp"), 0, keepdims=False)
     slot_out = summed.astype(jnp.bfloat16)
     row_max = lax.pmax(jnp.max(logits, axis=0), "expert")

time: 259 us -> 236 us (0.911)
  blocking collectives: 176 us -> 157 us
  waiting for transfers between devices: 48.5 us -> 45.1 us
    psum x1 -> x2, blocking collectives: 50.2 us -> 31 us  [on_device(): totals = lax.psum(totals, mesh_axis)]
    reduce_scatter x1, waiting for transfers between devices: 48.5 us -> 45.1 us  [on_device(): lax.psum_scatter(local_numer, 'expert', scatter_dimension=0, tiled=True)]
where the time goes in v1:
time: 236 us
  blocking collectives  157 us (67%)
  waiting for transfers between devices  45.1 us (19%)
  matrix products  15.6 us (7%)
  between operations  14.1 us (6%)
    reduce_scatter x1, waiting for transfers between devices, on_device(): lax.psum_scatter(local_numer, 'expert', scatter_dimension=0, tiled=True)  45.1 us
    unnamed x1, blocking collectives  40.5 us
    pmax x1, blocking collectives, on_device(): row_max = lax.pmax(jnp.max(logits, axis=0), 'expert')  37.7 us
    psum x2, blocking collectives, on_device(): totals = lax.psum(totals, mesh_axis)  31 us
    psum x1, blocking collectives, on_device(): numer_seq, denom_seq = lax.psum((numerator, denominator), 'seq')  27.1 us
    pmax x1, blocking collectives, on_device(): slot_max = lax.pmax(jnp.max(logits, axis=1), 'seq')  19 us
  transfers between devices with their start and end apart: 1, of which 1 were waited for; matrix products, arithmetic and copies ran while one was open for 0% of the time, Pallas kernels for 0%

profile of v1, /device:TPU:2, one launch (start us, length us, event | category | flops | bytes accessed | tf_op | source)
XLA Modules:
  0.0 235.9 jit_solution(13495031032659298869)
XLA Ops:
  6.5 0.0 copy-start
  6.5 0.0 reduce-scatter.2.cloned.1.call-start
  6.5 0.7 copy-done
  7.2 3.5 %fusion.35 = (f32[1024]{0:T(1024)S(1)}, f32[2]{0:T(128)S(1)}, f32[2,1024]{1,0:T(2,128)S(1)}) fusion(bf16[2048,2]{0,1:T(2,128)(2,1)S(1)} %copy-done, bf16[1024,2048]{1,0:T(8,128)(2,1)} %param.4), kind=kOutput, calls=%fused_computation.35 | convolution fusion | flops 8391678 | bytes 4214792 | tf_op jit(solution)/shard_map/dot_general | solution.py:8
  10.7 37.7 %pmax.14 = f32[1024]{0:T(1024)S(1)} all-reduce(f32[1024]{0:T(1024)S(1)} %get-tuple-element.7), channel_id=1, replica_groups=mesh['dp'=2,'seq'=8,'expert'=16] {'expert'}, use_global_device_ids=true, to_apply=%region_1.0 | all-reduce | flops 1024 | bytes 8192 | tf_op jit(solution)/shard_map/pmax | solution.py:28
  48.4 19.0 %pmax.15 = f32[2]{0:T(128)S(1)} all-reduce(f32[2]{0:T(128)S(1)} %get-tuple-element.8), channel_id=1, replica_groups=mesh['dp'=2,'seq'=8,'expert'=16] {'seq'}, use_global_device_ids=true, to_apply=%region_3.0 | all-reduce | flops 2 | bytes 16 | tf_op jit(solution)/shard_map/pmax | solution.py:11
  67.4 2.9 %fusion.23 = f32[2,2048]{1,0:T(2,128)S(1)} fusion(bf16[1024,2048]{1,0:T(8,128)(2,1)} %param.4, f32[2,1024]{1,0:T(2,128)S(1)} %get-tuple-element.11, f32[2]{0:T(128)S(1)} %pmax.15), kind=kOutput, calls=%fused_computation.25 | convolution fusion | flops 8392704 | bytes 4218888 | tf_op jit(solution)/shard_map/dot_general | solution.py:13
  70.3 0.2 fusion.19
  70.5 27.1 %all-reduce.1 = (f32[2,2048]{1,0:T(2,128)S(1)}, f32[2]{0:T(128)S(1)}) all-reduce(f32[2,2048]{1,0:T(2,128)S(1)} %fusion.23, f32[2]{0:T(128)S(1)} %get-tuple-element.6), channel_id=1, replica_groups=mesh['dp'=2,'seq'=8,'expert'=16] {'seq'}, use_global_device_ids=true, to_apply=%region_4.0 | all-reduce | flops 4098 | bytes 32784 | tf_op jit(solution)/shard_map/psum | solution.py:15
  97.6 0.1 fusion.18
  97.6 1.8 all-gather.1
  99.4 4.7 %convolution_bitcast_fusion = f32[2,2,2048]{2,0,1:T(2,128)S(1)} fusion(bf16[2,512,2048]{2,1,0:T(8,128)(2,1)} %param.7, bf16[2,2048,512]{2,1,0:T(8,128)(2,1)} %param.6, bf16[2,2,2048]{2,1,0:T(2,128)(2,1)S(1)} %all-gather.1), kind=kOutput, calls=%fused_computation | convolution fusion | flops 16795648 | bytes 8437760 | tf_op jit(solution)/shard_map/cef,efd->ced/dot_general | solution.py:22
  104.1 3.4 %psum.30 = f32[2,2,2048]{2,0,1:T(2,128)S(1)} all-reduce(f32[2,2,2048]{2,0,1:T(2,128)S(1)} %convolution_bitcast_fusion), channel_id=1, replica_groups=mesh['dp'=2,'seq'=8,'expert'=16] {'dp'}, use_global_device_ids=true, to_apply=%region_7.8 | all-reduce | flops 8192 | bytes 65536 | tf_op jit(solution)/shard_map/psum | solution.py:25
  107.5 27.6 %psum.31 = bf16[2,2,2048]{2,0,1:T(2,128)(2,1)S(1)} all-reduce(f32[2,2,2048]{2,0,1:T(2,128)S(1)} %psum.30), channel_id=1, replica_groups=mesh['dp'=2,'seq'=8,'expert'=16] {'seq'}, use_global_device_ids=true, to_apply=%region_8.9 | all-reduce | flops 8192 | bytes 49152 | tf_op jit(solution)/shard_map/psum | solution.py:25
  135.1 4.5 %fusion.15 = f32[1024,2048]{1,0:T(8,128)} fusion(bf16[1,2,2048]{2,0,1:T(2,128)(2,1)S(1)} %dynamic-slice_convert_fusion, f32[2,1024]{1,0:T(2,128)S(1)} %get-tuple-element.11, f32[1024]{0:T(1024)S(1)} %pmax.14), kind=kOutput, calls=%fused_computation.15 | convolution fusion | flops 8392704 | bytes 8409088 | tf_op jit(solution)/shard_map/dot_general | solution.py:30
  139.7 0.0 copy-start.1
  139.7 0.0 reduce-scatter.2.cloned.1.call-update
  139.7 0.6 copy-done.1
  140.3 0.6 dynamic-slice
  141.6 40.5 %all-reduce = f32[1024]{0:T(1024)S(1)} all-reduce(f32[1024]{0:T(1024)S(1)} %get-tuple-element.5), channel_id=4, replica_groups=mesh['dp'=2,'seq'=8,'expert'=16] {'expert'}, use_global_device_ids=true, to_apply=%region_11.12.clone | all-reduce | flops 1024 | bytes 8192
  182.0 0.1 dynamic-slice.1
  182.1 45.1 %reduce-scatter.2.cloned.1.call-done = f32[64,2048]{1,0:T(8,128)} async-done(((f32[1024,2048]{1,0:T(8,128)}), f32[64,2048]{1,0:T(8,128)}) %reduce-scatter.2.cloned.1.call-update) | async-done | bytes 524304 | tf_op jit(solution)/shard_map/reduce_scatter | solution.py:37
  227.2 1.8 divide_convert_fusion
  (1 shorter events, 0.0 us)
Async XLA Ops:
  6.5 0.7 copy-start
  6.5 220.6 %reduce-scatter.2.cloned.1.call-start = ((), (), s32[]{:S(2)}) async-start(), calls=%async_computation.1 | async-start | bytes 8912896 | tf_op jit(solution)/shard_map/reduce_scatter | solution.py:37
  139.7 0.7 copy-start.1
Sparse Core Ops, SparseCore 0:
  139.8 87.3 reduce-scatter.1
